TPU v7x, 32 devices: a whole 2x2x4 slice. The times are simulated.
32 devices in a mesh: tensor: 4 (over z), shard: 2 (over y), replica: 4 (over x, core).
Axes of the slice: x: 2, y: 2, z: 4, core: 2. Of those that a mesh axis runs over, the one named last changes fastest.
Arguments:
- block_in: float32 [8, 640, 1024], P(('shard', 'replica'), 'tensor'), may hold values from -12 to 12
- segment_ids: int32 [8, 640], P(('shard', 'replica')), may hold values from 0 to 3, never falling along the last dimension, each value on 1 to 256 neighbouring positions
- grad_out: float32 [8, 640, 1024], P(('shard', 'replica'), 'tensor'), may hold values from -6 to 6
- qkv_weight: bfloat16 [1024, 3, 1024], P('shard', None, 'tensor'), may hold values from -2 to 2
- qv_bias: bfloat16 [2, 1024], P(None, ('tensor', 'shard')), may hold values from -3 to 3
- out_weight: bfloat16 [1024, 1024], P('tensor', 'shard'), may hold values from -0.75 to 0.75
- up_weight: bfloat16 [1024, 4096], P('shard', 'tensor'), may hold values from -0.1875 to 0.1875
- up_bias: bfloat16 [4096], P(('tensor', 'shard')), may hold values from -3 to 3
- down_weight: bfloat16 [4096, 1024], P('tensor', 'shard'), may hold values from -0.09375 to 0.09375
- norm_gains: bfloat16 [2, 1024], P(None, 'shard'), may hold values from 0.25 to 1.75
- shift_biases: bfloat16 [4, 1024], P(None, 'shard'), may hold values from -3 to 3
Outputs:
- block_out: float32 [8, 640, 1024], P(('shard', 'replica'), 'tensor')
- grad_in: float32 [8, 640, 1024], P(('shard', 'replica'), 'tensor')
- grad_qkv_weight: float32 [1024, 3, 1024], P('shard', None, 'tensor')
- grad_qv_bias: float32 [2, 1024], P(None, ('tensor', 'shard'))
- grad_out_weight: float32 [1024, 1024], P('tensor', 'shard')
- grad_up_weight: float32 [1024, 4096], P('shard', 'tensor')
- grad_up_bias: float32 [4096], P(('tensor', 'shard'))
- grad_down_weight: float32 [4096, 1024], P('tensor', 'shard')
- grad_norm_gains: float32 [2, 1024], P(None, 'shard')
- grad_shift_biases: float32 [4, 1024], P(None, 'shard')
Inputs may be any that keep to these rules, and one draw needn't show every extreme that they name: segment_ids never fall along a sequence; a document has 1 to 256 tokens, and one has exactly 256.
All inputs are finite; a program needn't handle non-finite values.
Results may differ from a plain program's by a relative error of at most 0.009.
The roundings to bfloat16 on the way count: a program that leaves them out, or rounds other values in their place, can miss the bound.
Values may be sent and summed in bfloat16 or wider, within the bound.
A program may use at most 128 MiB of HBM per device.

v0:
```python
import math
import jax
import jax.numpy as jnp
from jax import lax
from jax.sharding import PartitionSpec as P

HEAD_DIM = 64
norm_eps = 1e-12
masked_score = -1e30


def norm_forward(summed, gain, shift):
    center = summed - jnp.mean(summed, axis=-1, keepdims=True)
    inverse = lax.rsqrt(jnp.mean(center * center, axis=-1, keepdims=True) + norm_eps)
    normed = center * inverse
    return (normed * gain + shift, normed, inverse)


def norm_backward(grad, normed, inverse, gain):
    scaled = grad * gain
    return inverse * (
        scaled
        - jnp.mean(scaled, axis=-1, keepdims=True)
        - normed * jnp.mean(scaled * normed, axis=-1, keepdims=True)
    )


def gelu_parts(pre_act):
    cumul = 0.5 * (1.0 + jax.scipy.special.erf(pre_act * 0.7071067811865476))
    density = jnp.exp(-0.5 * pre_act * pre_act) * 0.3989422804014327
    return (pre_act * cumul, cumul + pre_act * density)


def scatter_sum(part, axes, dim):
    return lax.psum_scatter(part.astype(jnp.bfloat16), axes, scatter_dimension=dim, tiled=True)


def shards(
    block_in,
    segment_ids,
    grad_out,
    qkv_weight,
    qv_bias,
    out_weight,
    up_weight,
    up_bias,
    down_weight,
    norm_gains,
    shift_biases,
):
    small = (qv_bias, up_bias[None], norm_gains, shift_biases)
    packed = lax.all_gather(jnp.concatenate([vec.reshape(-1) for vec in small]), "shard", axis=0)
    unpacked = []
    start = 0
    for vec in small:
        rows, piece = vec.shape
        part = packed[:, start : start + rows * piece].reshape(-1, rows, piece)
        unpacked.append(jnp.swapaxes(part, 0, 1).reshape(rows, -1))
        start += rows * piece
    qv_packed, upbias_packed, gain_packed, shift_packed = unpacked
    upbias_packed = upbias_packed[0]
    (
        query_key_value_full,
        qv_all,
        output_weight_full,
        up_weight_full,
        upbias_all,
        down_weight_full,
        gain_all,
        shift_all,
    ) = (
        lax.all_gather(qkv_weight, "shard", axis=0, tiled=True),
        qv_packed,
        lax.all_gather(out_weight, "shard", axis=1, tiled=True),
        lax.all_gather(up_weight, "shard", axis=0, tiled=True),
        upbias_packed,
        lax.all_gather(down_weight, "shard", axis=1, tiled=True),
        gain_packed,
        shift_packed,
    )
    seqs = block_in.shape[0]
    width = block_in.shape[2]
    length = segment_ids.shape[1]
    cols = query_key_value_full.shape[2]
    heads_here = cols // HEAD_DIM
    scale = 1.0 / math.sqrt(HEAD_DIM)
    gain_full = gain_all.astype(jnp.float32)
    shift_full = shift_all.astype(jnp.float32)
    qv_full = qv_all.astype(jnp.float32)
    inputs_bf = block_in.astype(jnp.bfloat16)
    input_rows_full = lax.all_gather(inputs_bf, "tensor", axis=1, tiled=True)
    query_key_value = jnp.einsum(
        "agp,pmy->agmy", input_rows_full, query_key_value_full, preferred_element_type=jnp.float32
    )
    query = (
        (query_key_value[:, :, 0] + qv_full[0])
        .astype(jnp.bfloat16)
        .reshape(seqs, length, heads_here, HEAD_DIM)
    )
    keys = query_key_value[:, :, 1].astype(jnp.bfloat16).reshape(seqs, length, heads_here, HEAD_DIM)
    values = (
        (query_key_value[:, :, 2] + qv_full[1])
        .astype(jnp.bfloat16)
        .reshape(seqs, length, heads_here, HEAD_DIM)
    )
    same = (segment_ids[:, :, None] == segment_ids[:, None, :])[:, None]
    scores = jnp.einsum("sqhe,skhe->shqk", query, keys, preferred_element_type=jnp.float32) * scale
    scores = jnp.where(same, scores, masked_score)
    highest = jnp.max(scores, axis=-1, keepdims=True)
    expo = jnp.exp(scores - highest)
    total = jnp.sum(expo, axis=-1, keepdims=True)
    probs = (expo / total).astype(jnp.bfloat16)
    log_total = highest + jnp.log(total)
    attention_context = jnp.einsum(
        "shqk,skhe->sqhe", probs, values, preferred_element_type=jnp.float32
    )
    attention_context = attention_context.astype(jnp.bfloat16).reshape(seqs, length, cols)
    attention_slice = jnp.einsum(
        "nip,pr->nir", attention_context, output_weight_full, preferred_element_type=jnp.float32
    )
    attended = scatter_sum(attention_slice, "tensor", 1).astype(jnp.float32)
    first_sum = block_in + (attended + shift_full[0])
    hidden, normed_one, inverse_one = norm_forward(first_sum, gain_full[0], shift_full[1])
    hidden_bf = hidden.astype(jnp.bfloat16)
    hidden_state_full = lax.all_gather(hidden_bf, "tensor", axis=1, tiled=True)
    pre_act = jnp.einsum(
        "peo,ot->pet", hidden_state_full, up_weight_full, preferred_element_type=jnp.float32
    ) + upbias_all.astype(jnp.float32)
    activ, slope = gelu_parts(pre_act)
    activation_bfloat = activ.astype(jnp.bfloat16)
    down_weight_slice = jnp.einsum(
        "uzt,tv->uzv", activation_bfloat, down_weight_full, preferred_element_type=jnp.float32
    )
    second_sum = hidden + (
        scatter_sum(down_weight_slice, "tensor", 1).astype(jnp.float32) + shift_full[2]
    )
    block_out, normed_two, inverse_two = norm_forward(second_sum, gain_full[1], shift_full[3])
    d_second = norm_backward(grad_out, normed_two, inverse_two, gain_full[1])
    second_gradient_full = lax.all_gather(
        d_second.astype(jnp.bfloat16), "tensor", axis=1, tiled=True
    )
    down_weight_gradient = jnp.einsum(
        "bct,bcm->tm", activation_bfloat, second_gradient_full, preferred_element_type=jnp.float32
    )
    d_pre = (
        jnp.einsum(
            "ajn,tn->ajt",
            second_gradient_full,
            down_weight_full,
            preferred_element_type=jnp.float32,
        )
        * slope
    )
    g_upbias = jnp.sum(d_pre, axis=(0, 1))
    preact_gradient_bfloat = d_pre.astype(jnp.bfloat16)
    up_weight_gradient = jnp.einsum(
        "ahk,ahp->kp", hidden_state_full, preact_gradient_bfloat, preferred_element_type=jnp.float32
    )
    hidden_state_slice = jnp.einsum(
        "ixj,gj->ixg", preact_gradient_bfloat, up_weight_full, preferred_element_type=jnp.float32
    )
    d_hidden = scatter_sum(hidden_state_slice, "tensor", 1).astype(jnp.float32) + d_second
    d_first = norm_backward(d_hidden, normed_one, inverse_one, gain_full[0])
    gain_part = jnp.stack(
        [jnp.sum(d_hidden * normed_one, axis=(0, 1)), jnp.sum(grad_out * normed_two, axis=(0, 1))]
    )
    shift_part = jnp.stack(
        [
            jnp.sum(d_first, axis=(0, 1)),
            jnp.sum(d_hidden, axis=(0, 1)),
            jnp.sum(d_second, axis=(0, 1)),
            jnp.sum(grad_out, axis=(0, 1)),
        ]
    )
    first_gradient_full = lax.all_gather(d_first.astype(jnp.bfloat16), "tensor", axis=1, tiled=True)
    output_weight_gradient = jnp.einsum(
        "unb,una->ba", attention_context, first_gradient_full, preferred_element_type=jnp.float32
    )
    context_gradient = jnp.einsum(
        "tbu,wu->tbw", first_gradient_full, output_weight_full, preferred_element_type=jnp.float32
    )
    context_gradient = context_gradient.astype(jnp.bfloat16).reshape(
        seqs, length, heads_here, HEAD_DIM
    )
    probs_back = jnp.exp(scores - log_total)
    d_probs = jnp.einsum(
        "sqhe,skhe->shqk", context_gradient, values, preferred_element_type=jnp.float32
    )
    row_dot = jnp.sum(probs_back * d_probs, axis=-1, keepdims=True)
    d_scores = (probs_back * (d_probs - row_dot)).astype(jnp.bfloat16)
    d_query = (
        jnp.einsum("shqk,skhe->sqhe", d_scores, keys, preferred_element_type=jnp.float32) * scale
    )
    d_keys = (
        jnp.einsum("shqk,sqhe->skhe", d_scores, query, preferred_element_type=jnp.float32) * scale
    )
    d_values = jnp.einsum(
        "shqk,sqhe->skhe",
        probs_back.astype(jnp.bfloat16),
        context_gradient,
        preferred_element_type=jnp.float32,
    )
    d_query = d_query.reshape(seqs, length, cols)
    d_keys = d_keys.reshape(seqs, length, cols)
    d_values = d_values.reshape(seqs, length, cols)
    g_qv = jnp.stack([jnp.sum(d_query, axis=(0, 1)), jnp.sum(d_values, axis=(0, 1))])
    projected_gradient_bfloat = jnp.stack([d_query, d_keys, d_values], axis=2).astype(jnp.bfloat16)
    projection_weight_gradient = jnp.einsum(
        "pjx,pjvy->xvy",
        input_rows_full,
        projected_gradient_bfloat,
        preferred_element_type=jnp.float32,
    )
    input_slice = jnp.einsum(
        "pxvk,yvk->pxy",
        projected_gradient_bfloat,
        query_key_value_full,
        preferred_element_type=jnp.float32,
    )
    grad_in = scatter_sum(input_slice, "tensor", 1).astype(jnp.float32) + d_first
    matrices = (
        projection_weight_gradient,
        output_weight_gradient,
        up_weight_gradient,
        down_weight_gradient,
    )
    spread = (
        scatter_sum(matrices[0], ("shard", "replica"), 0),
        scatter_sum(matrices[1], ("shard", "replica"), 1),
        scatter_sum(matrices[2], ("shard", "replica"), 0),
        scatter_sum(matrices[3], ("shard", "replica"), 1),
    )
    summed = (
        lax.all_gather(spread[0], "replica", axis=0, tiled=True).astype(jnp.float32),
        lax.all_gather(spread[1], "replica", axis=1, tiled=True).astype(jnp.float32),
        lax.all_gather(spread[2], "replica", axis=0, tiled=True).astype(jnp.float32),
        lax.all_gather(spread[3], "replica", axis=1, tiled=True).astype(jnp.float32),
    )
    tensor_index = lax.axis_index("tensor")
    shard_index = lax.axis_index("shard")
    shard_count = lax.axis_size("shard")
    tensor_count = lax.axis_size("tensor")
    upbias_width = upbias_all.shape[0]
    qv_wide = lax.dynamic_update_slice(
        jnp.zeros((2, width), jnp.float32), g_qv, (0, tensor_index * cols)
    )
    upbias_wide = lax.dynamic_update_slice(
        jnp.zeros((upbias_width * tensor_count,), jnp.float32),
        g_upbias,
        (tensor_index * upbias_width,),
    )
    gain_tot, shift_tot, qv_tot, upbias_tot = lax.psum(
        (gain_part, shift_part, qv_wide, upbias_wide), ("tensor", "shard", "replica")
    )
    vec_piece = norm_gains.shape[1]
    qv_piece = qv_bias.shape[1]
    upbias_piece = up_bias.shape[0]
    owner_index = tensor_index * shard_count + shard_index
    grad_gains = lax.dynamic_slice_in_dim(gain_tot, shard_index * vec_piece, vec_piece, 1)
    grad_shifts = lax.dynamic_slice_in_dim(shift_tot, shard_index * vec_piece, vec_piece, 1)
    grad_qv = lax.dynamic_slice_in_dim(qv_tot, owner_index * qv_piece, qv_piece, 1)
    grad_upbias = lax.dynamic_slice_in_dim(upbias_tot, owner_index * upbias_piece, upbias_piece, 0)
    return (
        block_out,
        grad_in,
        summed[0],
        grad_qv,
        summed[1],
        summed[2],
        grad_upbias,
        summed[3],
        grad_gains,
        grad_shifts,
    )


def solution(mesh):
    in_specs = (
        P(("shard", "replica"), "tensor", None),
        P(("shard", "replica"), None),
        P(("shard", "replica"), "tensor", None),
        P("shard", None, "tensor"),
        P(None, ("tensor", "shard")),
        P("tensor", "shard"),
        P("shard", "tensor"),
        P(("tensor", "shard")),
        P("tensor", "shard"),
        P(None, "shard"),
        P(None, "shard"),
    )
    out_specs = (
        P(("shard", "replica"), "tensor", None),
        P(("shard", "replica"), "tensor", None),
        P("shard", None, "tensor"),
        P(None, ("tensor", "shard")),
        P("tensor", "shard"),
        P("shard", "tensor"),
        P(("tensor", "shard")),
        P("tensor", "shard"),
        P(None, "shard"),
        P(None, "shard"),
    )
    return jax.shard_map(shards, mesh=mesh, in_specs=in_specs, out_specs=out_specs, check_vma=False)
```

profile of v0, /device:TPU:0, one launch (start us, length us, event | category | flops | bytes accessed | tf_op | source)
XLA Modules:
  0.0 611.5 jit_solution(1188588645892185024)
XLA Ops:
  10.7 5.4 all-gather.1
  16.3 12.0 %all_gather.46 = bf16[256,1024]{1,0:T(8,128)(2,1)S(1)} all-gather(bf16[256,512]{1,0:T(8,128)(2,1)S(1)} %copy-done.16), channel_id=1, replica_groups=mesh['tensor'=4,'shard'=2,'replica'=4] {'shard'}, dimensions={1}, use_global_device_ids=true | all-gather | bytes 786432 | tf_op jit(solution)/shard_map/all_gather | solution.py:74
  28.6 12.7 %all-gather.14.cloned.1.call-done = bf16[1024,3,256]{0,2,1:T(8,128)(2,1)} async-done(((bf16[512,3,256]{0,2,1:T(8,128)(2,1)}), bf16[1024,3,256]{0,2,1:T(8,128)(2,1)}) %all-gather.14.cloned.1.call-update) | async-done | bytes 1572880 | tf_op jit(solution)/shard_map/all_gather | solution.py:72
  41.3 36.2 %all-gather.12.cloned.1.call-done = bf16[1,640,1024]{2,1,0:T(8,128)(2,1)} async-done(((bf16[1,160,1024]{2,1,0:T(8,128)(2,1)}), bf16[1,640,1024]{2,1,0:T(8,128)(2,1)}) %all-gather.12.cloned.1.call-update) | async-done | bytes 1310736 | tf_op jit(solution)/shard_map/all_gather | solution.py:91
  77.4 3.2 convolution_bitcast_fusion
  89.4 29.9 %reduce-scatter.15.cloned.1.call-done = bf16[1,160,1024]{2,1,0:T(8,128)(2,1)} async-done(((bf16[1,640,1024]{2,1,0:T(8,128)(2,1)}), bf16[1,160,1024]{2,1,0:T(8,128)(2,1)}) %reduce-scatter.15.cloned.1.call-update) | async-done | bytes 327696 | tf_op jit(solution)/shard_map/reduce_scatter | solution.py:35
  122.2 30.2 %all-gather.18.cloned.1.call-done = bf16[1024,1024]{1,0:T(8,128)(2,1)} async-done(((bf16[512,1024]{1,0:T(8,128)(2,1)}), bf16[1024,1024]{1,0:T(8,128)(2,1)}) %all-gather.18.cloned.1.call-update) | async-done | bytes 2097168 | tf_op jit(solution)/shard_map/all_gather | solution.py:75
  152.4 34.5 %all-gather.16.cloned.1.call-done = bf16[1,640,1024]{2,1,0:T(8,128)(2,1)} async-done(((bf16[1,160,1024]{2,1,0:T(8,128)(2,1)}), bf16[1,640,1024]{2,1,0:T(8,128)(2,1)}) %all-gather.16.cloned.1.call-update) | async-done | bytes 1310736 | tf_op jit(solution)/shard_map/all_gather | solution.py:125
  187.0 5.2 multiply_convert_fusion.1
  192.2 28.4 %all-gather.20.cloned.1.call-done = bf16[1024,1024]{1,0:T(8,128)(2,1)} async-done(((bf16[1024,512]{1,0:T(8,128)(2,1)}), bf16[1024,1024]{1,0:T(8,128)(2,1)}) %all-gather.20.cloned.1.call-update) | async-done | bytes 2097168 | tf_op jit(solution)/shard_map/all_gather | solution.py:77
  220.6 4.2 fusion.12
  224.9 31.5 %reduce-scatter.17.cloned.1.call-done = bf16[1,160,1024]{2,1,0:T(8,128)(2,1)} async-done(((bf16[1,640,1024]{2,1,0:T(8,128)(2,1)}), bf16[1,160,1024]{2,1,0:T(8,128)(2,1)}) %reduce-scatter.17.cloned.1.call-update) | async-done | bytes 327696 | tf_op jit(solution)/shard_map/reduce_scatter | solution.py:35
  260.2 31.1 %all-gather.22.cloned.1.call-done = bf16[1,640,1024]{2,1,0:T(8,128)(2,1)} async-done(((bf16[1,160,1024]{2,1,0:T(8,128)(2,1)}), bf16[1,640,1024]{2,1,0:T(8,128)(2,1)}) %all-gather.22.cloned.1.call-update) | async-done | bytes 1310736 | tf_op jit(solution)/shard_map/all_gather | solution.py:139
  291.4 5.9 fusion.55
  301.0 4.9 convolution_convert_fusion.1
  305.9 3.6 convolution_convert_fusion
  312.2 19.4 %reduce-scatter.19.cloned.1.call-done = bf16[1,160,1024]{2,1,0:T(8,128)(2,1)} async-done(((bf16[1,640,1024]{2,1,0:T(8,128)(2,1)}), bf16[1,160,1024]{2,1,0:T(8,128)(2,1)}) %reduce-scatter.19.cloned.1.call-update) | async-done | bytes 327696 | tf_op jit(solution)/shard_map/reduce_scatter | solution.py:35
  337.4 37.6 %reduce-scatter.23.cloned.1.call-done = bf16[128,1024]{1,0:T(8,128)(2,1)} async-done(((bf16[1024,1024]{1,0:T(8,128)(2,1)}), bf16[128,1024]{1,0:T(8,128)(2,1)}) %reduce-scatter.23.cloned.1.call-update) | async-done | bytes 262160 | tf_op jit(solution)/shard_map/reduce_scatter | solution.py:35
  375.2 44.9 %reduce-scatter.29.cloned.1.call-done = bf16[128,1024]{1,0:T(8,128)(2,1)} async-done(((bf16[1024,1024]{1,0:T(8,128)(2,1)}), bf16[128,1024]{1,0:T(8,128)(2,1)}) %reduce-scatter.29.cloned.1.call-update) | async-done | bytes 262160
  422.0 32.7 %all-gather.24.cloned.1.call-done = bf16[1,640,1024]{2,1,0:T(8,128)(2,1)} async-done(((bf16[1,160,1024]{2,1,0:T(8,128)(2,1)}), bf16[1,640,1024]{2,1,0:T(8,128)(2,1)}) %all-gather.24.cloned.1.call-update) | async-done | bytes 1310736 | tf_op jit(solution)/shard_map/all_gather | solution.py:175
  459.8 5.0 fusion.51
  464.8 4.0 multiply_reduce_fusion
  469.2 6.0 multiply_convert_fusion
  480.4 3.1 fusion.33
  484.6 3.0 convolution_convert_fusion.2
  489.3 3.7 fusion.11
  493.6 40.0 %all-reduce = (f32[2,1024]{1,0:T(2,128)S(1)}, f32[4096]{0:T(1024)S(1)}, f32[2,1024]{1,0:T(2,128)S(1)}, f32[4,1024]{1,0:T(4,128)S(1)}) all-reduce(f32[2,1024]{1,0:T(2,128)S(1)} %maximum_dynamic-update-slice_fusion, f32[4096]{0:T(1024)S(1)} %dynamic_update_slice.7, ...), channel_id=1, replica_groups=mesh['tensor'=4,'shard'=2,'replica'=4] {'tensor','shard','replica'}, use_global_device_ids=true, to_apply=%region_18.19 | all-reduce | flops 12288 | bytes 98304 | tf_op jit(solution)/shard_map/psum | solution.py:252
  538.8 2.9 convert_element_type.225
  542.7 6.5 %all_gather.53 = bf16[256,512]{1,0:T(8,128)(2,1)S(1)} all-gather(bf16[256,128]{1,0:T(8,128)(2,1)S(1)} %copy.63), channel_id=1, replica_groups=mesh['tensor'=4,'shard'=2,'replica'=4] {'replica'}, dimensions={1}, use_global_device_ids=true | all-gather | bytes 327680 | tf_op jit(solution)/shard_map/all_gather | solution.py:235
  550.0 19.5 %reduce-scatter.25.cloned.1.call-done = bf16[128,768]{1,0:T(8,128)(2,1)} async-done(((bf16[1024,768]{1,0:T(8,128)(2,1)}), bf16[128,768]{1,0:T(8,128)(2,1)}) %reduce-scatter.25.cloned.1.call-update) | async-done | bytes 196624
  570.6 8.6 %all_gather.52 = bf16[512,3,256]{0,2,1:T(8,128)(2,1)S(1)} all-gather(bf16[128,3,256]{0,2,1:T(8,128)(2,1)S(1)} %bitcast.140), channel_id=1, replica_groups=mesh['tensor'=4,'shard'=2,'replica'=4] {'replica'}, dimensions={0}, use_global_device_ids=true | all-gather | bytes 983040 | tf_op jit(solution)/shard_map/all_gather | solution.py:234
  580.6 22.5 %reduce-scatter.21.cloned.1.call-done = bf16[1,160,1024]{2,1,0:T(8,128)(2,1)} async-done(((bf16[1,640,1024]{2,1,0:T(8,128)(2,1)}), bf16[1,160,1024]{2,1,0:T(8,128)(2,1)}) %reduce-scatter.21.cloned.1.call-update) | async-done | bytes 327696 | tf_op jit(solution)/shard_map/reduce_scatter | solution.py:35
  (193 shorter events, 58.7 us)
Async XLA Ops:
  7.2 9.1 %copy-start.31 = (s32[1,640]{1,0:T(1,128)S(1)}, s32[1,640]{1,0:T(1,128)}, u32[]{:S(2)}) copy-start(s32[1,640]{1,0:T(1,128)} %param.12) | copy-start | bytes 7684
  7.2 9.1 %copy-start.16 = (bf16[256,512]{1,0:T(8,128)(2,1)S(1)}, bf16[256,512]{1,0:T(8,128)(2,1)}, u32[]{:S(2)}) copy-start(bf16[256,512]{1,0:T(8,128)(2,1)} %param.16) | copy-start | bytes 786436
  7.2 34.0 %all-gather.14.cloned.1.call-start = ((), (), s32[]{:S(2)}) async-start(), calls=%async_computation.9 | async-start | bytes 2359296 | tf_op jit(solution)/shard_map/all_gather | solution.py:72
  9.7 67.8 %all-gather.12.cloned.1.call-start = ((), (), s32[]{:S(2)}) async-start(), calls=%async_computation.8 | async-start | bytes 1638400 | tf_op jit(solution)/shard_map/all_gather | solution.py:91
  10.5 108.7 %reduce-scatter.15.cloned.1.call-start = ((), (), s32[]{:S(2)}) async-start(), calls=%async_computation.10 | async-start | bytes 1638400 | tf_op jit(solution)/shard_map/reduce_scatter | solution.py:35
  16.2 66.9 %copy-start.27 = (f32[4,64]{1,0:T(4,128)}, f32[4,64]{1,0:T(4,128)S(1)}, u32[]{:S(2)}) copy-start(f32[4,64]{1,0:T(4,128)S(1)} %add.169) | copy-start | bytes 3076
  28.3 58.0 %copy-start.11 = (bf16[256,1024]{1,0:T(8,128)(2,1)}, bf16[256,1024]{1,0:T(8,128)(2,1)S(1)}, u32[]{:S(2)}) copy-start(bf16[256,1024]{1,0:T(8,128)(2,1)S(1)} %all_gather.46) | copy-start | bytes 1572868
  88.6 63.8 %all-gather.18.cloned.1.call-start = ((), (), s32[]{:S(2)}) async-start(), calls=%async_computation.12 | async-start | bytes 3145728 | tf_op jit(solution)/shard_map/all_gather | solution.py:75
  89.2 97.8 %all-gather.16.cloned.1.call-start = ((), (), s32[]{:S(2)}) async-start(), calls=%async_computation.11 | async-start | bytes 1638400 | tf_op jit(solution)/shard_map/all_gather | solution.py:125
  121.6 99.1 %all-gather.20.cloned.1.call-start = ((), (), s32[]{:S(2)}) async-start(), calls=%async_computation.13 | async-start | bytes 3145728 | tf_op jit(solution)/shard_map/all_gather | solution.py:77
  122.1 134.2 %reduce-scatter.17.cloned.1.call-start = ((), (), s32[]{:S(2)}) async-start(), calls=%async_computation.14 | async-start | bytes 1638400 | tf_op jit(solution)/shard_map/reduce_scatter | solution.py:35
  192.2 28.4 %copy-start.36 = (bf16[640,1024]{1,0:T(8,128)(2,1)}, bf16[640,1024]{1,0:T(8,128)(2,1)S(1)}, u32[]{:S(2)}) copy-start(bf16[640,1024]{1,0:T(8,128)(2,1)S(1)} %get-tuple-element.78) | copy-start | bytes 3932164
  224.8 33.1 %copy-start.10 = (f32[1,160,1024]{2,1,0:T(8,128)S(1)}, f32[1,160,1024]{2,1,0:T(8,128)}, u32[]{:S(2)}) copy-start(f32[1,160,1024]{2,1,0:T(8,128)} %param.13) | copy-start | bytes 1966084
  224.8 66.5 %all-gather.22.cloned.1.call-start = ((), (), s32[]{:S(2)}) async-start(), calls=%async_computation.15 | async-start | bytes 1638400 | tf_op jit(solution)/shard_map/all_gather | solution.py:139
  260.0 71.6 %copy-start.4 = (f32[1,160,1024]{2,1,0:T(8,128)}, f32[1,160,1024]{2,1,0:T(8,128)S(1)}, u32[]{:S(2)}) copy-start(f32[1,160,1024]{2,1,0:T(8,128)S(1)} %get-tuple-element.58) | copy-start | bytes 1966084
  260.0 71.6 %reduce-scatter.19.cloned.1.call-start = ((), (), s32[]{:S(2)}) async-start(), calls=%async_computation.16 | async-start | bytes 1638400 | tf_op jit(solution)/shard_map/reduce_scatter | solution.py:35
  291.4 6.9 %copy-start.35 = (bf16[1024,1024]{1,0:T(8,128)(2,1)S(1)}, bf16[1024,1024]{1,0:T(8,128)(2,1)}, u32[]{:S(2)}) copy-start(bf16[1024,1024]{1,0:T(8,128)(2,1)} %all-gather.18.cloned.1.call-done) | copy-start | bytes 6291460
  300.9 74.1 %reduce-scatter.23.cloned.1.call-start = ((), (), s32[]{:S(2)}) async-start(), calls=%async_computation.19 | async-start | bytes 2359296 | tf_op jit(solution)/shard_map/reduce_scatter | solution.py:35
  305.9 114.2 %reduce-scatter.29.cloned.1.call-start = ((), (), s32[]{:S(2)}) async-start(), calls=%async_computation.24 | async-start | bytes 2359296
  312.1 142.5 %all-gather.24.cloned.1.call-start = ((), (), s32[]{:S(2)}) async-start(), calls=%async_computation.17 | async-start | bytes 1638400 | tf_op jit(solution)/shard_map/all_gather | solution.py:175
  333.6 131.2 %slice-start = ((s8[6553600]{0:T(1024)(128)(4,1)}), s8[2359296]{0:T(1024)(128)(4,1)S(1)}, s32[]{:S(2)}) async-start(s8[6553600]{0:T(1024)(128)(4,1)} %bitcast.122), calls=%async_computation.25 | async-start | bytes 4718592
  335.8 86.2 %copy-start.18 = (f32[4,640]{1,0:T(4,128)S(1)}, f32[4,640]{1,0:T(4,128)}, u32[]{:S(2)}) copy-start(f32[4,640]{1,0:T(4,128)} %copy-done.17) | copy-start | bytes 30724
  335.8 86.2 %copy-start.20 = (f32[4,640]{1,0:T(4,128)S(1)}, f32[4,640]{1,0:T(4,128)}, u32[]{:S(2)}) copy-start(f32[4,640]{1,0:T(4,128)} %copy-done.19) | copy-start | bytes 30724
  337.4 198.6 %all-gather.26.cloned.1.call-start = ((), (), s32[]{:S(2)}) async-start(), calls=%async_computation.20 | async-start | bytes 1310720 | tf_op jit(solution)/shard_map/all_gather | solution.py:236
  375.1 82.6 %copy-start.12 = (bf16[256,1024]{1,0:T(8,128)(2,1)S(1)}, bf16[256,1024]{1,0:T(8,128)(2,1)}, u32[]{:S(2)}) copy-start(bf16[256,1024]{1,0:T(8,128)(2,1)} %copy-done.11) | copy-start | bytes 1572868
  375.1 163.7 %all-gather.28.cloned.1.call-start = ((), (), s32[]{:S(2)}) async-start(), calls=%async_computation.21 | async-start | bytes 1310720 | tf_op jit(solution)/shard_map/all_gather | solution.py:237
  421.9 119.8 %reduce-scatter.27.cloned.1.call-start = ((), (), s32[]{:S(2)}) async-start(), calls=%async_computation.23 | async-start | bytes 589824
  457.7 7.1 %slice-start.1 = ((s8[6553600]{0:T(1024)(128)(4,1)}), s8[4194304]{0:T(1024)(128)(4,1)S(1)}, s32[]{:S(2)}) async-start(s8[6553600]{0:T(1024)(128)(4,1)} %bitcast.122), calls=%async_computation.26 | async-start | bytes 8388608
  468.9 100.6 %reduce-scatter.25.cloned.1.call-start = ((), (), s32[]{:S(2)}) async-start(), calls=%async_computation.22 | async-start | bytes 1769472
  469.2 6.0 copy-start.6
  489.2 113.8 %reduce-scatter.21.cloned.1.call-start = ((), (), s32[]{:S(2)}) async-start(), calls=%async_computation.18 | async-start | bytes 1638400 | tf_op jit(solution)/shard_map/reduce_scatter | solution.py:35
  549.1 53.9 %copy-start.3 = (f32[1,160,1024]{2,1,0:T(8,128)S(1)}, f32[1,160,1024]{2,1,0:T(8,128)}, u32[]{:S(2)}) copy-start(f32[1,160,1024]{2,1,0:T(8,128)} %copy-done.2) | copy-start | bytes 1966084
  (25 other events, 74.9 us)
Sparse Core Ops, SparseCore 0:
  10.2 31.0 all-gather.13
  43.4 33.9 all-gather.11
  88.7 30.4 reduce-scatter.14
  120.6 31.7 all-gather.17
  154.4 32.5 all-gather.15
  188.4 32.1 all-gather.19
  224.9 31.3 reduce-scatter.16
  260.1 31.1 all-gather.21
  301.1 30.4 reduce-scatter.18
  335.3 39.7 reduce-scatter.22
  378.9 41.1 reduce-scatter.28
  422.1 32.5 all-gather.23
  456.2 15.7 all-gather.25
  473.5 16.8 all-gather.27
  493.2 34.1 reduce-scatter.26
  531.1 38.3 reduce-scatter.24
  571.6 31.3 reduce-scatter.20
where the time goes:
time: 612 us; the launch traced here: 611 us
  waiting for transfers between devices  412 us (67%)
  blocking collectives  72.4 us (12%)
  matrix products  58.1 us (9%)
  other arithmetic  27.4 us (4%)
  local copies, waits for them, and re-layouts  25.5 us (4%)
  between operations  14.7 us (2%)
    reduce_scatter x5, waiting for transfers between devices, scatter_sum(): lax.psum_scatter(part.astype(jnp.bfloat16), axes, scatter_dimension=dim,...  141 us
    unnamed x20, waiting for transfers between devices  65.7 us
    psum x1, blocking collectives, shards(): lax.psum((gain_part, shift_part, qv_wide, upbias_wide), ('tensor', 'shard...  40 us
    all_gather x1, waiting for transfers between devices, shards(): input_rows_full = lax.all_gather(inputs_bf, 'tensor', axis=1, tiled=True)  36.2 us
    all_gather x1, waiting for transfers between devices, shards(): hidden_state_full = lax.all_gather(hidden_bf, 'tensor', axis=1, tiled=True)  34.5 us
    all_gather x1, waiting for transfers between devices, shards(): lax.all_gather(d_first.astype(jnp.bfloat16), 'tensor', axis=1, tiled=True)  32.7 us
    all_gather x1, waiting for transfers between devices, shards(): lax.all_gather(d_second.astype(jnp.bfloat16), 'tensor', axis=1, tiled=True)  31.1 us
    all_gather x1, waiting for transfers between devices, shards(): lax.all_gather(up_weight, 'shard', axis=0, tiled=True)  30.2 us
  transfers between devices with their start and end apart: 17, of which 14 were waited for; matrix products, arithmetic and copies ran while one was open for 13% of the time, Pallas kernels for 0%

commit v1 on v0

--- a/solution.py
+++ b/solution.py
@@ -250,7 +250,8 @@
         (tensor_index * upbias_width,),
     )
     gain_tot, shift_tot, qv_tot, upbias_tot = lax.psum(
-        (gain_part, shift_part, qv_wide, upbias_wide), ("tensor", "shard", "replica")
+        lax.psum((gain_part, shift_part, qv_wide, upbias_wide), axis_name=("shard", "replica")),
+        axis_name="tensor",
     )
     vec_piece = norm_gains.shape[1]
     qv_piece = qv_bias.shape[1]

time: 612 us -> 612 us (level)
    psum x1 -> x2, blocking collectives: 40 us -> 42 us  [the longest x1 23.6 us: shards(): lax.psum((gain_part, shift_part, qv_wide, upbias_wide), axis_name=('shard...]
where the time goes in v1:
time: 612 us; the launch traced here: 611 us
  waiting for transfers between devices  411 us (67%)
  blocking collectives  73.8 us (12%)
  matrix products  58.1 us (9%)
  other arithmetic  27.4 us (4%)
  local copies, waits for them, and re-layouts  25.4 us (4%)
  between operations  14.7 us (2%)
    reduce_scatter x5, waiting for transfers between devices, scatter_sum(): lax.psum_scatter(part.astype(jnp.bfloat16), axes, scatter_dimension=dim,...  141 us
    unnamed x20, waiting for transfers between devices  64.3 us
    all_gather x1, waiting for transfers between devices, shards(): input_rows_full = lax.all_gather(inputs_bf, 'tensor', axis=1, tiled=True)  36.2 us
    all_gather x1, waiting for transfers between devices, shards(): hidden_state_full = lax.all_gather(hidden_bf, 'tensor', axis=1, tiled=True)  34.5 us
    all_gather x1, waiting for transfers between devices, shards(): lax.all_gather(d_first.astype(jnp.bfloat16), 'tensor', axis=1, tiled=True)  32.6 us
    all_gather x1, waiting for transfers between devices, shards(): lax.all_gather(d_second.astype(jnp.bfloat16), 'tensor', axis=1, tiled=True)  31.1 us
    all_gather x1, waiting for transfers between devices, shards(): lax.all_gather(up_weight, 'shard', axis=0, tiled=True)  30.2 us
    all_gather x1, waiting for transfers between devices, shards(): lax.all_gather(down_weight, 'shard', axis=1, tiled=True)  28.4 us
  transfers between devices with their start and end apart: 17, of which 14 were waited for; matrix products, arithmetic and copies ran while one was open for 13% of the time, Pallas kernels for 0%

profile of v1, /device:TPU:0, one launch (start us, length us, event | category | flops | bytes accessed | tf_op | source)
XLA Modules:
  0.0 611.4 jit_solution(1714323254327031873)
XLA Ops:
  10.7 5.4 all-gather.1
  16.3 12.0 %all_gather.46 = bf16[256,1024]{1,0:T(8,128)(2,1)S(1)} all-gather(bf16[256,512]{1,0:T(8,128)(2,1)S(1)} %copy-done.16), channel_id=1, replica_groups=mesh['tensor'=4,'shard'=2,'replica'=4] {'shard'}, dimensions={1}, use_global_device_ids=true | all-gather | bytes 786432 | tf_op jit(solution)/shard_map/all_gather | solution.py:74
  28.6 12.7 %all-gather.14.cloned.1.call-done = bf16[1024,3,256]{0,2,1:T(8,128)(2,1)} async-done(((bf16[512,3,256]{0,2,1:T(8,128)(2,1)}), bf16[1024,3,256]{0,2,1:T(8,128)(2,1)}) %all-gather.14.cloned.1.call-update) | async-done | bytes 1572880 | tf_op jit(solution)/shard_map/all_gather | solution.py:72
  41.3 36.2 %all-gather.12.cloned.1.call-done = bf16[1,640,1024]{2,1,0:T(8,128)(2,1)} async-done(((bf16[1,160,1024]{2,1,0:T(8,128)(2,1)}), bf16[1,640,1024]{2,1,0:T(8,128)(2,1)}) %all-gather.12.cloned.1.call-update) | async-done | bytes 1310736 | tf_op jit(solution)/shard_map/all_gather | solution.py:91
  77.4 3.2 convolution_bitcast_fusion
  89.3 29.9 %reduce-scatter.15.cloned.1.call-done = bf16[1,160,1024]{2,1,0:T(8,128)(2,1)} async-done(((bf16[1,640,1024]{2,1,0:T(8,128)(2,1)}), bf16[1,160,1024]{2,1,0:T(8,128)(2,1)}) %reduce-scatter.15.cloned.1.call-update) | async-done | bytes 327696 | tf_op jit(solution)/shard_map/reduce_scatter | solution.py:35
  122.2 30.2 %all-gather.18.cloned.1.call-done = bf16[1024,1024]{1,0:T(8,128)(2,1)} async-done(((bf16[512,1024]{1,0:T(8,128)(2,1)}), bf16[1024,1024]{1,0:T(8,128)(2,1)}) %all-gather.18.cloned.1.call-update) | async-done | bytes 2097168 | tf_op jit(solution)/shard_map/all_gather | solution.py:75
  152.4 34.5 %all-gather.16.cloned.1.call-done = bf16[1,640,1024]{2,1,0:T(8,128)(2,1)} async-done(((bf16[1,160,1024]{2,1,0:T(8,128)(2,1)}), bf16[1,640,1024]{2,1,0:T(8,128)(2,1)}) %all-gather.16.cloned.1.call-update) | async-done | bytes 1310736 | tf_op jit(solution)/shard_map/all_gather | solution.py:125
  187.0 5.2 multiply_convert_fusion.1
  192.2 28.4 %all-gather.20.cloned.1.call-done = bf16[1024,1024]{1,0:T(8,128)(2,1)} async-done(((bf16[1024,512]{1,0:T(8,128)(2,1)}), bf16[1024,1024]{1,0:T(8,128)(2,1)}) %all-gather.20.cloned.1.call-update) | async-done | bytes 2097168 | tf_op jit(solution)/shard_map/all_gather | solution.py:77
  220.6 4.2 fusion.12
  224.8 31.5 %reduce-scatter.17.cloned.1.call-done = bf16[1,160,1024]{2,1,0:T(8,128)(2,1)} async-done(((bf16[1,640,1024]{2,1,0:T(8,128)(2,1)}), bf16[1,160,1024]{2,1,0:T(8,128)(2,1)}) %reduce-scatter.17.cloned.1.call-update) | async-done | bytes 327696 | tf_op jit(solution)/shard_map/reduce_scatter | solution.py:35
  260.2 31.1 %all-gather.22.cloned.1.call-done = bf16[1,640,1024]{2,1,0:T(8,128)(2,1)} async-done(((bf16[1,160,1024]{2,1,0:T(8,128)(2,1)}), bf16[1,640,1024]{2,1,0:T(8,128)(2,1)}) %all-gather.22.cloned.1.call-update) | async-done | bytes 1310736 | tf_op jit(solution)/shard_map/all_gather | solution.py:139
  291.3 5.9 fusion.55
  301.0 4.9 convolution_convert_fusion.1
  305.9 3.6 convolution_convert_fusion
  312.2 19.4 %reduce-scatter.19.cloned.1.call-done = bf16[1,160,1024]{2,1,0:T(8,128)(2,1)} async-done(((bf16[1,640,1024]{2,1,0:T(8,128)(2,1)}), bf16[1,160,1024]{2,1,0:T(8,128)(2,1)}) %reduce-scatter.19.cloned.1.call-update) | async-done | bytes 327696 | tf_op jit(solution)/shard_map/reduce_scatter | solution.py:35
  337.4 37.6 %reduce-scatter.23.cloned.1.call-done = bf16[128,1024]{1,0:T(8,128)(2,1)} async-done(((bf16[1024,1024]{1,0:T(8,128)(2,1)}), bf16[128,1024]{1,0:T(8,128)(2,1)}) %reduce-scatter.23.cloned.1.call-update) | async-done | bytes 262160 | tf_op jit(solution)/shard_map/reduce_scatter | solution.py:35
  375.1 45.0 %reduce-scatter.29.cloned.1.call-done = bf16[128,1024]{1,0:T(8,128)(2,1)} async-done(((bf16[1024,1024]{1,0:T(8,128)(2,1)}), bf16[128,1024]{1,0:T(8,128)(2,1)}) %reduce-scatter.29.cloned.1.call-update) | async-done | bytes 262160
  422.0 32.6 %all-gather.24.cloned.1.call-done = bf16[1,640,1024]{2,1,0:T(8,128)(2,1)} async-done(((bf16[1,160,1024]{2,1,0:T(8,128)(2,1)}), bf16[1,640,1024]{2,1,0:T(8,128)(2,1)}) %all-gather.24.cloned.1.call-update) | async-done | bytes 1310736 | tf_op jit(solution)/shard_map/all_gather | solution.py:175
  459.7 5.0 fusion.51
  464.8 4.0 multiply_reduce_fusion
  469.1 6.0 multiply_convert_fusion
  480.3 3.1 fusion.33
  484.5 3.0 convolution_convert_fusion.2
  489.3 3.7 fusion.11
  493.6 23.6 %all-reduce = (f32[2,1024]{1,0:T(2,128)S(1)}, f32[4096]{0:T(1024)S(1)}, f32[2,1024]{1,0:T(2,128)S(1)}, f32[4,1024]{1,0:T(4,128)S(1)}) all-reduce(f32[2,1024]{1,0:T(2,128)S(1)} %maximum_dynamic-update-slice_fusion, f32[4096]{0:T(1024)S(1)} %dynamic_update_slice.7, ...), channel_id=1, replica_groups=mesh['tensor'=4,'shard'=2,'replica'=4] {'shard','replica'}, use_global_device_ids=true, to_apply=%region_18.19 | all-reduce | flops 12288 | bytes 98304 | tf_op jit(solution)/shard_map/psum | solution.py:253
  517.1 18.4 %all-reduce.1 = (f32[2,1024]{1,0:T(2,128)S(1)}, f32[4096]{0:T(1024)S(1)}, f32[2,1024]{1,0:T(2,128)S(1)}, f32[4,1024]{1,0:T(4,128)S(1)}) all-reduce(f32[2,1024]{1,0:T(2,128)S(1)} %get-tuple-element.51, f32[4096]{0:T(1024)S(1)} %get-tuple-element.52, ...), channel_id=1, replica_groups=mesh['tensor'=4,'shard'=2,'replica'=4] {'tensor'}, use_global_device_ids=true, to_apply=%region_19.20 | all-reduce | flops 12288 | bytes 98304 | tf_op jit(solution)/shard_map/psum | solution.py:252
  544.7 5.8 all_gather.53
  551.3 18.1 %reduce-scatter.25.cloned.1.call-done = bf16[128,768]{1,0:T(8,128)(2,1)} async-done(((bf16[1024,768]{1,0:T(8,128)(2,1)}), bf16[128,768]{1,0:T(8,128)(2,1)}) %reduce-scatter.25.cloned.1.call-update) | async-done | bytes 196624
  570.5 8.6 %all_gather.52 = bf16[512,3,256]{0,2,1:T(8,128)(2,1)S(1)} all-gather(bf16[128,3,256]{0,2,1:T(8,128)(2,1)S(1)} %bitcast.140), channel_id=1, replica_groups=mesh['tensor'=4,'shard'=2,'replica'=4] {'replica'}, dimensions={0}, use_global_device_ids=true | all-gather | bytes 983040 | tf_op jit(solution)/shard_map/all_gather | solution.py:234
  580.5 22.5 %reduce-scatter.21.cloned.1.call-done = bf16[1,160,1024]{2,1,0:T(8,128)(2,1)} async-done(((bf16[1,640,1024]{2,1,0:T(8,128)(2,1)}), bf16[1,160,1024]{2,1,0:T(8,128)(2,1)}) %reduce-scatter.21.cloned.1.call-update) | async-done | bytes 327696 | tf_op jit(solution)/shard_map/reduce_scatter | solution.py:35
  (194 shorter events, 61.6 us)
Async XLA Ops:
  7.2 9.1 %copy-start.31 = (s32[1,640]{1,0:T(1,128)S(1)}, s32[1,640]{1,0:T(1,128)}, u32[]{:S(2)}) copy-start(s32[1,640]{1,0:T(1,128)} %param.12) | copy-start | bytes 7684
  7.2 9.1 %copy-start.16 = (bf16[256,512]{1,0:T(8,128)(2,1)S(1)}, bf16[256,512]{1,0:T(8,128)(2,1)}, u32[]{:S(2)}) copy-start(bf16[256,512]{1,0:T(8,128)(2,1)} %param.16) | copy-start | bytes 786436
  7.2 34.0 %all-gather.14.cloned.1.call-start = ((), (), s32[]{:S(2)}) async-start(), calls=%async_computation.9 | async-start | bytes 2359296 | tf_op jit(solution)/shard_map/all_gather | solution.py:72
  9.7 67.8 %all-gather.12.cloned.1.call-start = ((), (), s32[]{:S(2)}) async-start(), calls=%async_computation.8 | async-start | bytes 1638400 | tf_op jit(solution)/shard_map/all_gather | solution.py:91
  10.5 108.7 %reduce-scatter.15.cloned.1.call-start = ((), (), s32[]{:S(2)}) async-start(), calls=%async_computation.10 | async-start | bytes 1638400 | tf_op jit(solution)/shard_map/reduce_scatter | solution.py:35
  16.2 66.9 %copy-start.27 = (f32[4,64]{1,0:T(4,128)}, f32[4,64]{1,0:T(4,128)S(1)}, u32[]{:S(2)}) copy-start(f32[4,64]{1,0:T(4,128)S(1)} %add.177) | copy-start | bytes 3076
  28.3 58.0 %copy-start.11 = (bf16[256,1024]{1,0:T(8,128)(2,1)}, bf16[256,1024]{1,0:T(8,128)(2,1)S(1)}, u32[]{:S(2)}) copy-start(bf16[256,1024]{1,0:T(8,128)(2,1)S(1)} %all_gather.46) | copy-start | bytes 1572868
  88.6 63.8 %all-gather.18.cloned.1.call-start = ((), (), s32[]{:S(2)}) async-start(), calls=%async_computation.12 | async-start | bytes 3145728 | tf_op jit(solution)/shard_map/all_gather | solution.py:75
  89.2 97.8 %all-gather.16.cloned.1.call-start = ((), (), s32[]{:S(2)}) async-start(), calls=%async_computation.11 | async-start | bytes 1638400 | tf_op jit(solution)/shard_map/all_gather | solution.py:125
  121.5 99.1 %all-gather.20.cloned.1.call-start = ((), (), s32[]{:S(2)}) async-start(), calls=%async_computation.13 | async-start | bytes 3145728 | tf_op jit(solution)/shard_map/all_gather | solution.py:77
  122.1 134.2 %reduce-scatter.17.cloned.1.call-start = ((), (), s32[]{:S(2)}) async-start(), calls=%async_computation.14 | async-start | bytes 1638400 | tf_op jit(solution)/shard_map/reduce_scatter | solution.py:35
  192.2 28.4 %copy-start.36 = (bf16[640,1024]{1,0:T(8,128)(2,1)}, bf16[640,1024]{1,0:T(8,128)(2,1)S(1)}, u32[]{:S(2)}) copy-start(bf16[640,1024]{1,0:T(8,128)(2,1)S(1)} %get-tuple-element.82) | copy-start | bytes 3932164
  224.8 33.1 %copy-start.10 = (f32[1,160,1024]{2,1,0:T(8,128)S(1)}, f32[1,160,1024]{2,1,0:T(8,128)}, u32[]{:S(2)}) copy-start(f32[1,160,1024]{2,1,0:T(8,128)} %param.13) | copy-start | bytes 1966084
  224.8 66.5 %all-gather.22.cloned.1.call-start = ((), (), s32[]{:S(2)}) async-start(), calls=%async_computation.15 | async-start | bytes 1638400 | tf_op jit(solution)/shard_map/all_gather | solution.py:139
  260.0 71.6 %copy-start.4 = (f32[1,160,1024]{2,1,0:T(8,128)}, f32[1,160,1024]{2,1,0:T(8,128)S(1)}, u32[]{:S(2)}) copy-start(f32[1,160,1024]{2,1,0:T(8,128)S(1)} %get-tuple-element.62) | copy-start | bytes 1966084
  260.0 71.6 %reduce-scatter.19.cloned.1.call-start = ((), (), s32[]{:S(2)}) async-start(), calls=%async_computation.16 | async-start | bytes 1638400 | tf_op jit(solution)/shard_map/reduce_scatter | solution.py:35
  291.3 6.9 %copy-start.35 = (bf16[1024,1024]{1,0:T(8,128)(2,1)S(1)}, bf16[1024,1024]{1,0:T(8,128)(2,1)}, u32[]{:S(2)}) copy-start(bf16[1024,1024]{1,0:T(8,128)(2,1)} %all-gather.18.cloned.1.call-done) | copy-start | bytes 6291460
  300.9 74.1 %reduce-scatter.23.cloned.1.call-start = ((), (), s32[]{:S(2)}) async-start(), calls=%async_computation.19 | async-start | bytes 2359296 | tf_op jit(solution)/shard_map/reduce_scatter | solution.py:35
  305.9 114.2 %reduce-scatter.29.cloned.1.call-start = ((), (), s32[]{:S(2)}) async-start(), calls=%async_computation.24 | async-start | bytes 2359296
  312.1 142.5 %all-gather.24.cloned.1.call-start = ((), (), s32[]{:S(2)}) async-start(), calls=%async_computation.17 | async-start | bytes 1638400 | tf_op jit(solution)/shard_map/all_gather | solution.py:175
  333.6 131.2 %slice-start = ((s8[6553600]{0:T(1024)(128)(4,1)}), s8[2359296]{0:T(1024)(128)(4,1)S(1)}, s32[]{:S(2)}) async-start(s8[6553600]{0:T(1024)(128)(4,1)} %bitcast.122), calls=%async_computation.25 | async-start | bytes 4718592
  335.8 86.2 %copy-start.18 = (f32[4,640]{1,0:T(4,128)S(1)}, f32[4,640]{1,0:T(4,128)}, u32[]{:S(2)}) copy-start(f32[4,640]{1,0:T(4,128)} %copy-done.17) | copy-start | bytes 30724
  335.8 86.2 %copy-start.20 = (f32[4,640]{1,0:T(4,128)S(1)}, f32[4,640]{1,0:T(4,128)}, u32[]{:S(2)}) copy-start(f32[4,640]{1,0:T(4,128)} %copy-done.19) | copy-start | bytes 30724
  337.4 200.6 %all-gather.26.cloned.1.call-start = ((), (), s32[]{:S(2)}) async-start(), calls=%async_computation.20 | async-start | bytes 1310720 | tf_op jit(solution)/shard_map/all_gather | solution.py:236
  375.1 82.6 %copy-start.12 = (bf16[256,1024]{1,0:T(8,128)(2,1)S(1)}, bf16[256,1024]{1,0:T(8,128)(2,1)}, u32[]{:S(2)}) copy-start(bf16[256,1024]{1,0:T(8,128)(2,1)} %copy-done.11) | copy-start | bytes 1572868
  375.1 165.7 %all-gather.28.cloned.1.call-start = ((), (), s32[]{:S(2)}) async-start(), calls=%async_computation.21 | async-start | bytes 1310720 | tf_op jit(solution)/shard_map/all_gather | solution.py:237
  421.9 121.8 %reduce-scatter.27.cloned.1.call-start = ((), (), s32[]{:S(2)}) async-start(), calls=%async_computation.23 | async-start | bytes 589824
  457.6 7.1 %slice-start.1 = ((s8[6553600]{0:T(1024)(128)(4,1)}), s8[4194304]{0:T(1024)(128)(4,1)S(1)}, s32[]{:S(2)}) async-start(s8[6553600]{0:T(1024)(128)(4,1)} %bitcast.122), calls=%async_computation.26 | async-start | bytes 8388608
  468.9 100.6 %reduce-scatter.25.cloned.1.call-start = ((), (), s32[]{:S(2)}) async-start(), calls=%async_computation.22 | async-start | bytes 1769472
  469.1 6.0 copy-start.6
  489.2 113.8 %reduce-scatter.21.cloned.1.call-start = ((), (), s32[]{:S(2)}) async-start(), calls=%async_computation.18 | async-start | bytes 1638400 | tf_op jit(solution)/shard_map/reduce_scatter | solution.py:35
  550.5 52.5 %copy-start.3 = (f32[1,160,1024]{2,1,0:T(8,128)S(1)}, f32[1,160,1024]{2,1,0:T(8,128)}, u32[]{:S(2)}) copy-start(f32[1,160,1024]{2,1,0:T(8,128)} %copy-done.2) | copy-start | bytes 1966084
  (25 other events, 75.0 us)
Sparse Core Ops, SparseCore 0:
  10.2 31.0 all-gather.13
  43.4 33.9 all-gather.11
  88.7 30.4 reduce-scatter.14
  120.6 31.7 all-gather.17
  154.4 32.5 all-gather.15
  188.4 32.1 all-gather.19
  224.9 31.3 reduce-scatter.16
  260.1 31.1 all-gather.21
  301.1 30.4 reduce-scatter.18
  335.3 39.7 reduce-scatter.22
  378.9 41.1 reduce-scatter.28
  422.1 32.4 all-gather.23
  456.2 15.7 all-gather.25
  473.4 16.8 all-gather.27
  493.2 34.1 reduce-scatter.26
  531.1 38.3 reduce-scatter.24
  571.6 31.3 reduce-scatter.20
